TPU v7x, 512 devices: a whole 4x4x16 slice. The times are simulated.
512 devices in a mesh: gx: 32 (over y, z_lo), gy: 16 (over x, z_hi, core).
Axes of the slice: x: 4, y: 4, z: 16 (z_hi: 2, z_lo: 8; z = z_hi * 8 + z_lo), core: 2. Of those that a mesh axis runs over, the one named last changes fastest.
Arguments:
- mass_per_volume: float32 [1024, 8192], P('gy', 'gx'), may hold values from 0.5 to 2
- motion_speed: float32 [1024, 3, 8192], P('gy', None, 'gx'), may hold values from -3 to 3
- agitation_energy: float32 [1024, 8192], P('gy', 'gx'), may hold values from 0.5 to 2
- shear_deviatoric: float32 [1024, 5, 8192], P('gy', None, 'gx'), may hold values from -2.4 to 2.4
- thermal_current_array: float32 [1024, 3, 8192], P('gy', None, 'gx'), may hold values from -2.4 to 2.4
Outputs:
- rate: float32 [1024, 13, 8192], P('gy', None, 'gx')
All inputs are finite; a program needn't handle non-finite values.
Results may differ from a plain program's by a relative error of at most 0.0043.
The roundings to bfloat16 on the way count: a program that leaves them out, or rounds other values in their place, can miss the bound.
Values may be sent and summed in bfloat16 or wider, within the bound.
A program may use at most 64 MiB of HBM per device.

v0:
```python
import math

import jax
import jax.numpy as jnp
from jax import lax
from jax.sharding import PartitionSpec as P

CROSS_NODES = 1024


time_step = 0.05
enforcement_weight = 4.0
plate_speed = 0.5
dissipation_speed = 0.25


def extended(shard, sides, width):
    for axis, dim in sides:
        count, length = (lax.axis_size(axis), shard.shape[dim])
        up = [(i, (i + 1) % count) for i in range(count)]
        down = [(j, i) for i, j in up]
        last = lax.slice_in_dim(shard, length - width, length, axis=dim)
        initial = lax.slice_in_dim(shard, 0, width, axis=dim)
        before = lax.ppermute(last, axis, up)
        after = lax.ppermute(initial, axis, down)
        shard = jnp.concatenate([before, shard, after], axis=dim)
    return shard


def derivative_rows(first, count, size):
    last = size - 1
    half = math.pi / (2.0 * last)
    rows = first + jnp.arange(count, dtype=jnp.int32)
    cols = jnp.arange(size, dtype=jnp.int32)
    summed = (rows[:, None] + cols[None, :]).astype(jnp.float32)
    differ = rows[:, None] - cols[None, :]
    same = differ == 0
    denom = -2.0 * jnp.sin(half * summed) * jnp.sin(half * differ.astype(jnp.float32))
    safe = jnp.where(same, jnp.float32(1.0), denom)

    def weights(index):
        edge = jnp.where((index == 0) | (index == last), jnp.float32(2.0), jnp.float32(1.0))
        parity = (1 - 2 * (index % 2)).astype(jnp.float32)
        return edge * parity

    ratio = weights(rows)[:, None] / weights(cols)[None, :]
    scale = math.pi / last * jnp.sin(2.0 * half * rows.astype(jnp.float32))
    offdiag = jnp.where(same, jnp.float32(0.0), scale[:, None] * ratio / safe)
    diagonal = -jnp.sum(offdiag, axis=1)
    return (offdiag + jnp.where(same, diagonal[:, None], jnp.float32(0.0))).astype(jnp.bfloat16)


def fluxes(unknown_collection):
    agitation_energy = unknown_collection[:, 4]
    motion_speed = [unknown_collection[:, 1], unknown_collection[:, 2], unknown_collection[:, 3]]
    traction_matrix = [
        [unknown_collection[:, 5], unknown_collection[:, 6], unknown_collection[:, 8]],
        [unknown_collection[:, 6], unknown_collection[:, 7], unknown_collection[:, 9]],
        [
            unknown_collection[:, 8],
            unknown_collection[:, 9],
            -(unknown_collection[:, 5] + unknown_collection[:, 7]),
        ],
    ]
    thermal_current_entry = [
        unknown_collection[:, 10],
        unknown_collection[:, 11],
        unknown_collection[:, 12],
    ]
    pairs = [(0, 0), (0, 1), (1, 1), (0, 2), (1, 2)]
    result = []
    for spatial_axis_number in (0, 1):
        transported_quantity = motion_speed[spatial_axis_number]
        local_quantity = [unknown_collection[:, 0] * transported_quantity]
        for leading_subscript in range(3):
            local_quantity.append(
                motion_speed[leading_subscript] * transported_quantity
                + traction_matrix[leading_subscript][spatial_axis_number]
                + (agitation_energy if leading_subscript == spatial_axis_number else 0.0)
            )
        local_quantity.append(
            transported_quantity * agitation_energy
            + 2.0 / 3.0 * thermal_current_entry[spatial_axis_number]
        )
        for leading_subscript, trailing_subscript in pairs:
            production_entry = (
                transported_quantity * traction_matrix[leading_subscript][trailing_subscript]
            )
            production_entry = production_entry + 0.4 * (
                (
                    thermal_current_entry[leading_subscript]
                    if trailing_subscript == spatial_axis_number
                    else 0.0
                )
                + (
                    thermal_current_entry[trailing_subscript]
                    if leading_subscript == spatial_axis_number
                    else 0.0
                )
            )
            production_entry = production_entry - (
                4.0 / 15.0 * thermal_current_entry[spatial_axis_number]
                if leading_subscript == trailing_subscript
                else 0.0
            )
            local_quantity.append(production_entry)
        for leading_subscript in range(3):
            local_quantity.append(
                transported_quantity * thermal_current_entry[leading_subscript]
                + agitation_energy * traction_matrix[leading_subscript][spatial_axis_number]
                + (
                    2.5 * agitation_energy * agitation_energy
                    if leading_subscript == spatial_axis_number
                    else 0.0
                )
            )
        result.append(jnp.stack(local_quantity, axis=1))
    return (result[0], result[1])


def source(unknown_collection, rows, size):
    mass_per_volume = unknown_collection[:, 0]
    agitation_energy = unknown_collection[:, 4]
    impact_often_measure = mass_per_volume * jnp.sqrt(agitation_energy * agitation_energy + 0.25)
    plate_condition = jnp.where(
        rows == 0,
        jnp.float32(1.0),
        jnp.where(rows == size - 1, jnp.float32(-1.0), jnp.float32(0.0)),
    )[:, None]
    radial_distribution = jnp.abs(plate_condition)
    blank_quantity = jnp.zeros_like(mass_per_volume)
    production_entries = [
        blank_quantity,
        -enforcement_weight
        * radial_distribution
        * (unknown_collection[:, 1] - plate_speed * plate_condition),
        blank_quantity,
        blank_quantity,
        -dissipation_speed * impact_often_measure * agitation_energy
        - enforcement_weight * radial_distribution * (agitation_energy - 1.0),
    ]
    production_entries = production_entries + [
        -0.8 * impact_often_measure * unknown_collection[:, k] for k in range(5, 10)
    ]
    production_entries = production_entries + [
        -0.55 * impact_often_measure * unknown_collection[:, k] for k in range(10, 13)
    ]
    return jnp.stack(production_entries, axis=1)


def streamwise(flux_x):
    padded = extended(flux_x, (("gx", 2),), 3)
    width = flux_x.shape[2]
    coeffs = (0.75, -0.15, 1.0 / 60.0)
    along = jnp.zeros_like(flux_x)
    for k in range(3):
        upper = padded[:, :, 4 + k : 4 + k + width]
        lower = padded[:, :, 2 - k : 2 - k + width]
        along = along + coeffs[k] * (upper - lower)
    return along


def wall_normal(lowered, grid):
    piece = lax.all_gather(lowered, "gy", axis=0, tiled=True)
    summed = jnp.dot(grid, piece.reshape(piece.shape[0], -1), preferred_element_type=jnp.float32)
    return summed.reshape(lowered.shape)


def section_rate(unknown_collection, grid, rows):
    flux_x, flux_y = fluxes(unknown_collection)
    along = streamwise(flux_x)
    across = wall_normal(flux_y.astype(jnp.bfloat16), grid)
    return -(along + across) + source(unknown_collection, rows, CROSS_NODES)


def on_device(
    mass_per_volume, motion_speed, agitation_energy, shear_deviatoric, thermal_current_array
):
    unknown_collection = jnp.concatenate(
        [
            mass_per_volume[:, None],
            motion_speed,
            agitation_energy[:, None],
            shear_deviatoric,
            thermal_current_array,
        ],
        axis=1,
    )
    height = unknown_collection.shape[0]
    first = lax.axis_index("gy") * height
    rows = first + jnp.arange(height, dtype=jnp.int32)
    grid = derivative_rows(first, height, CROSS_NODES)
    first_rate = section_rate(unknown_collection, grid, rows)
    middle = unknown_collection + time_step * first_rate
    second_rate = section_rate(middle, grid, rows)
    return 0.5 * (first_rate + second_rate)


def solution(mesh):
    return jax.shard_map(
        on_device,
        mesh=mesh,
        in_specs=(
            P("gy", "gx"),
            P("gy", None, "gx"),
            P("gy", "gx"),
            P("gy", None, "gx"),
            P("gy", None, "gx"),
        ),
        out_specs=P("gy", None, "gx"),
        check_vma=False,
    )
```

profile of v0, /device:TPU:1, one launch (start us, length us, event | category | flops | bytes accessed | tf_op | source)
XLA Modules:
  0.0 395.1 jit_solution(12346683918850810533)
XLA Ops:
  6.6 0.0 all-gather.3.cloned.1.call-start
  6.6 1.0 constant_dynamic-update-slice_fusion.25
  7.6 0.9 constant_dynamic-update-slice_fusion.24
  8.5 0.9 constant_dynamic-update-slice_fusion.23
  9.4 0.9 constant_dynamic-update-slice_fusion.22
  10.3 0.9 constant_dynamic-update-slice_fusion.21
  11.3 0.9 constant_dynamic-update-slice_fusion.20
  12.2 0.9 constant_dynamic-update-slice_fusion.19
  13.1 0.9 constant_dynamic-update-slice_fusion.18
  14.0 0.9 constant_dynamic-update-slice_fusion.17
  14.9 0.9 constant_dynamic-update-slice_fusion.16
  15.8 1.0 constant_dynamic-update-slice_fusion.15
  16.8 1.0 constant_dynamic-update-slice_fusion.14
  17.8 1.0 constant_dynamic-update-slice_fusion.13
  18.7 0.8 copy-done.5
  19.5 0.0 all-gather.3.cloned.1.call-update
  19.5 0.0 all-gather.5.cloned.1.call-start
  19.6 0.9 constant_dynamic-update-slice_fusion.42
  20.5 0.9 constant_dynamic-update-slice_fusion.11
  21.4 0.9 constant_dynamic-update-slice_fusion.10
  22.3 0.9 constant_dynamic-update-slice_fusion.9
  23.3 0.9 constant_dynamic-update-slice_fusion.8
  24.2 0.9 constant_dynamic-update-slice_fusion.7
  25.1 0.9 constant_dynamic-update-slice_fusion.6
  26.0 0.9 constant_dynamic-update-slice_fusion.5
  27.0 0.9 constant_dynamic-update-slice_fusion.4
  27.9 0.9 constant_dynamic-update-slice_fusion.3
  28.8 1.0 constant_dynamic-update-slice_fusion.2
  29.7 1.0 constant_dynamic-update-slice_fusion.1
  30.8 0.1 constant_dynamic-update-slice_fusion.34
  31.0 0.2 fusion.101
  31.1 16.1 %collective-permute-start = (f32[64,13,3]{2,0,1:T(8,128)S(1)}, f32[64,13,3]{2,0,1:T(8,128)}, u32[]{:S(2)}, u32[]{:S(2)}) collective-permute-start(f32[64,13,3]{2,0,1:T(8,128)S(1)} %get-tuple-element.18), channel_id=1, source_target_pairs={{16,0},{32,16},{48,32},{64,48},{80,64},{96,80},{112,96},{128,112},... | collective-permute-start | bytes 29960 | tf_op jit(solution)/shard_map/ppermute | solution.py:25
  47.3 1.9 collective-permute-start.1
  49.3 2.1 fusion.40
  51.6 0.9 copy-done.7
  52.5 135.7 %all-gather.3.cloned.1.call-done = bf16[1024,13,256]{2,0,1:T(8,128)(2,1)} async-done(((bf16[64,13,256]{2,0,1:T(8,128)(2,1)}), bf16[1024,13,256]{2,0,1:T(8,128)(2,1)}) %all-gather.3.cloned.1.call-update) | async-done | bytes 6815760 | tf_op jit(solution)/shard_map/all_gather | solution.py:164
  188.2 10.3 %copy.6 = bf16[1024,13,256]{0,2,1:T(8,128)(2,1)} copy(bf16[1024,13,256]{2,0,1:T(8,128)(2,1)} %all-gather.3.cloned.1.call-done) | data formatting | bytes 13631488 | tf_op jit(solution)/shard_map/all_gather | solution.py:164
  198.6 10.8 %multiply_add_fusion = (f32[64,13,256]{2,0,1:T(8,128)S(1)}, f32[64,13,256]{2,0,1:T(8,128)}) fusion(f32[64,13,256]{2,0,1:T(8,128)} %copy-done.7, f32[64,13,256]{2,0,1:T(8,128)S(1)} %constant_dynamic-update-slice_fusion.26, bf16[1024,13,256]{0,2,1:T(8,128)(2,1)} %copy.6, f32[64]{0:T(128)S(1)} %neg.13, s32[64]{0:T(128)S(1)} %iota_add_fusion, ...), kind=kOutput, calls=%fused_computation.56 | convolution fusion | flops 441368576 | bytes 11100672 | tf_op jit(solution)/shard_map/dot_general | solution.py:165
  209.7 0.8 copy-done.6
  210.4 0.0 all-gather.5.cloned.1.call-update
  210.7 0.1 constant_dynamic-update-slice_fusion.46
  210.8 0.1 constant_dynamic-update-slice_fusion.77
  211.0 0.2 fusion.100
  211.2 9.5 %collective-permute-start.2 = (f32[64,13,3]{2,0,1:T(8,128)S(1)}, f32[64,13,3]{2,0,1:T(8,128)}, u32[]{:S(2)}, u32[]{:S(2)}) collective-permute-start(f32[64,13,3]{2,0,1:T(8,128)S(1)} %get-tuple-element.9), channel_id=1, source_target_pairs={{16,0},{32,16},{48,32},{64,48},{80,64},{96,80},{112,96},{128,112},... | collective-permute-start | bytes 29960 | tf_op jit(solution)/shard_map/ppermute | solution.py:25
  220.7 2.1 collective-permute-start.3
  222.9 144.4 %all-gather.5.cloned.1.call-done = bf16[1024,13,256]{2,0,1:T(8,128)(2,1)} async-done(((bf16[64,13,256]{2,0,1:T(8,128)(2,1)}), bf16[1024,13,256]{2,0,1:T(8,128)(2,1)}) %all-gather.5.cloned.1.call-update) | async-done | bytes 6815760 | tf_op jit(solution)/shard_map/all_gather | solution.py:164
  367.3 10.3 %copy.7 = bf16[1024,13,256]{0,2,1:T(8,128)(2,1)} copy(bf16[1024,13,256]{2,0,1:T(8,128)(2,1)} %all-gather.5.cloned.1.call-done) | data formatting | bytes 13631488 | tf_op jit(solution)/shard_map/all_gather | solution.py:164
  377.6 10.6 %fusion.13 = f32[64,13,256]{2,0,1:T(8,128)} fusion(f32[64,13,256]{2,0,1:T(8,128)S(1)} %copy-done.8, f32[64,13,256]{2,0,1:T(8,128)S(1)} %constant_dynamic-update-slice_fusion.69, f32[64,13,256]{2,0,1:T(8,128)S(1)} %get-tuple-element.11, f32[64,13,3]{2,0,1:T(8,128)} %collective-permute-done.3, f32[64,13,3]{2,0,1:T(8,128)} %collective-permute-done.2, ...), kind=kOutput, calls=%fused_computation.29 | convolution fusion | flops 441368576 | bytes 10248704 | tf_op jit(solution)/shard_map/dot_general | solution.py:165
  (70 shorter events, 0.8 us)
Async XLA Ops:
  6.5 24.2 %copy-start = (f32[64,3,256]{2,0,1:T(8,128)S(1)}, f32[64,3,256]{2,0,1:T(8,128)}, u32[]{:S(2)}) copy-start(f32[64,3,256]{2,0,1:T(8,128)} %param.6) | copy-start | bytes 589828
  6.5 24.3 %copy-start.4 = (f32[64,256]{1,0:T(8,128)S(1)}, f32[64,256]{1,0:T(8,128)}, u32[]{:S(2)}) copy-start(f32[64,256]{1,0:T(8,128)} %param.5) | copy-start | bytes 196612
  6.5 24.4 %copy-start.1 = (f32[64,5,256]{2,0,1:T(8,128)S(1)}, f32[64,5,256]{2,0,1:T(8,128)}, u32[]{:S(2)}) copy-start(f32[64,5,256]{2,0,1:T(8,128)} %param.8) | copy-start | bytes 983044
  6.5 24.3 %copy-start.3 = (f32[64,256]{1,0:T(8,128)S(1)}, f32[64,256]{1,0:T(8,128)}, u32[]{:S(2)}) copy-start(f32[64,256]{1,0:T(8,128)} %param.7) | copy-start | bytes 196612
  6.5 24.4 %copy-start.2 = (f32[64,3,256]{2,0,1:T(8,128)S(1)}, f32[64,3,256]{2,0,1:T(8,128)}, u32[]{:S(2)}) copy-start(f32[64,3,256]{2,0,1:T(8,128)} %param.9) | copy-start | bytes 589828
  6.6 181.7 %all-gather.3.cloned.1.call-start = ((), (), s32[]{:S(2)}) async-start(), calls=%async_computation | async-start | bytes 7241728 | tf_op jit(solution)/shard_map/all_gather | solution.py:164
  18.7 0.8 copy-start.5
  19.5 347.8 %all-gather.5.cloned.1.call-start = ((), (), s32[]{:S(2)}) async-start(), calls=%async_computation.1 | async-start | bytes 7241728 | tf_op jit(solution)/shard_map/all_gather | solution.py:164
  31.1 167.4 %collective-permute-start = (f32[64,13,3]{2,0,1:T(8,128)S(1)}, f32[64,13,3]{2,0,1:T(8,128)}, u32[]{:S(2)}, u32[]{:S(2)}) collective-permute-start(f32[64,13,3]{2,0,1:T(8,128)S(1)} %get-tuple-element.18), channel_id=1, source_target_pairs={{16,0},{32,16},{48,32},{64,48},{80,64},{96,80},{112,96},{128,112},... | collective-permute-start | bytes 29960 | tf_op jit(solution)/shard_map/ppermute | solution.py:25
  47.3 151.2 %collective-permute-start.1 = (f32[64,13,3]{2,0,1:T(8,128)S(1)}, f32[64,13,3]{2,0,1:T(8,128)}, u32[]{:S(2)}, u32[]{:S(2)}) collective-permute-start(f32[64,13,3]{2,0,1:T(8,128)S(1)} %get-tuple-element.19), channel_id=1, source_target_pairs={{0,16},{16,32},{32,48},{48,64},{64,80},{80,96},{96,112},{112,128},... | collective-permute-start | bytes 29960 | tf_op jit(solution)/shard_map/ppermute | solution.py:24
  51.6 0.9 copy-start.7
  209.7 0.8 copy-start.6
  211.2 166.4 %collective-permute-start.2 = (f32[64,13,3]{2,0,1:T(8,128)S(1)}, f32[64,13,3]{2,0,1:T(8,128)}, u32[]{:S(2)}, u32[]{:S(2)}) collective-permute-start(f32[64,13,3]{2,0,1:T(8,128)S(1)} %get-tuple-element.9), channel_id=1, source_target_pairs={{16,0},{32,16},{48,32},{64,48},{80,64},{96,80},{112,96},{128,112},... | collective-permute-start | bytes 29960 | tf_op jit(solution)/shard_map/ppermute | solution.py:25
  220.7 156.8 %collective-permute-start.3 = (f32[64,13,3]{2,0,1:T(8,128)S(1)}, f32[64,13,3]{2,0,1:T(8,128)}, u32[]{:S(2)}, u32[]{:S(2)}) collective-permute-start(f32[64,13,3]{2,0,1:T(8,128)S(1)} %get-tuple-element.10), channel_id=1, source_target_pairs={{0,16},{16,32},{32,48},{48,64},{64,80},{80,96},{96,112},{112,128},... | collective-permute-start | bytes 29960 | tf_op jit(solution)/shard_map/ppermute | solution.py:24
  222.9 154.7 %copy-start.8 = (f32[64,13,256]{2,0,1:T(8,128)S(1)}, f32[64,13,256]{2,0,1:T(8,128)}, u32[]{:S(2)}) copy-start(f32[64,13,256]{2,0,1:T(8,128)} %get-tuple-element.28) | copy-start | bytes 2555908
Sparse Core Ops, SparseCore 0:
  19.6 168.5 all-gather.2
  210.6 156.6 all-gather.4
where the time goes:
time: 400 us; the launch traced here: 395 us
  waiting for transfers between devices  280 us (70%)
  starting transfers between devices  29.8 us (7%)
  other arithmetic  26.3 us (7%)
  local copies, waits for them, and re-layouts  23.5 us (6%)
  matrix products  21.5 us (5%)
  between operations  14 us (4%)
    all_gather x2, waiting for transfers between devices, wall_normal(): piece = lax.all_gather(lowered, 'gy', axis=0, tiled=True)  280 us
    ppermute x2, starting transfers between devices, extended(): after = lax.ppermute(initial, axis, down)  25.7 us
    unnamed x60, other arithmetic  23 us
    dot_general x2, matrix products, wall_normal(): jnp.dot(grid, piece.reshape(piece.shape[0], -1), preferred_element_type=j...  21.5 us
    all_gather x2, local copies, waits for them, and re-layouts, wall_normal(): piece = lax.all_gather(lowered, 'gy', axis=0, tiled=True)  20.6 us
  transfers between devices with their start and end apart: 6, of which 2 were waited for; matrix products, arithmetic and copies ran while one was open for 9% of the time, Pallas kernels for 0%

commit v1 on v0

v1 whole, which is shorter than its diff:
```python
import math

import jax
import jax.numpy as jnp
from jax import lax
from jax.experimental import pallas as pl
from jax.experimental.pallas import tpu as pltpu
from jax.sharding import PartitionSpec as P

CROSS_NODES = 1024
LAST = CROSS_NODES - 1
HALF = math.pi / (2.0 * LAST)
MESH = pl.DeviceIdType.MESH

time_step = 0.05
enforcement_weight = 4.0
plate_speed = 0.5
dissipation_speed = 0.25
coeffs = (0.75, -0.15, 1.0 / 60.0)

FIELDS = 13
ROWS = 64
COLS = 128
TILE = 16
PARTS = 4
LAG = 2

SPREAD = [(160.0, 1.25)] + [(40.0, 0.0)] * 3 + [(160.0, 1.25)] + [(50.0, 0.0)] * 8


def encode(value, field):
    rate, centre = SPREAD[field]
    return jnp.exp2(rate * (value - centre)).astype(jnp.bfloat16)


def decode(code, field):
    rate, centre = SPREAD[field]
    return jnp.log(code.astype(jnp.float32)) * (1.0 / (rate * math.log(2.0))) + centre


def flux(u, d):
    temp = u[4]
    speed = u[1:4]
    s = [[u[5], u[6], u[8]], [u[6], u[7], u[9]], [u[8], u[9], -(u[5] + u[7])]]
    q = u[10:13]
    carry = speed[d]
    out = [u[0] * carry]
    for i in range(3):
        term = speed[i] * carry + s[i][d]
        out.append(term + temp if i == d else term)
    out.append(carry * temp + (2.0 / 3.0) * q[d])
    for i, j in ((0, 0), (0, 1), (1, 1), (0, 2), (1, 2)):
        term = carry * s[i][j]
        if i == d and j == d:
            term = term + 0.8 * q[d]
        elif j == d:
            term = term + 0.4 * q[i]
        elif i == d:
            term = term + 0.4 * q[j]
        if i == j:
            term = term - (4.0 / 15.0) * q[d]
        out.append(term)
    for i in range(3):
        term = carry * q[i] + temp * s[i][d]
        out.append(term + 2.5 * temp * temp if i == d else term)
    return out


def source(u, wall):
    rate = u[0] * jnp.sqrt(u[4] * u[4] + 0.25)
    near = jnp.abs(wall)
    out = [None, -enforcement_weight * near * (u[1] - plate_speed * wall), None, None]
    out.append(-dissipation_speed * rate * u[4] - enforcement_weight * near * (u[4] - 1.0))
    out += [-0.8 * rate * u[k] for k in range(5, 10)]
    out += [-0.55 * rate * u[k] for k in range(10, 13)]
    return out


def stencil(f):
    total = None
    for k in range(3):
        term = coeffs[k] * (pltpu.roll(f, COLS - k - 1, 1) - pltpu.roll(f, k + 1, 1))
        total = term if total is None else total + term
    return total


def edges(f, lane):
    out = jnp.zeros_like(f[0])
    for m in range(FIELDS):
        a = pltpu.roll(f[m], 3 * m, 1) if m else f[m]
        out = jnp.where((lane >= 3 * m) & (lane < 3 * m + 3), a, out)
        b = pltpu.roll(f[m], 43 + 3 * m, 1)
        out = jnp.where((lane >= 40 + 3 * m) & (lane < 43 + 3 * m), b, out)
    return out


def mend(diff, lane):
    low = lane < 40
    place = jnp.where(low, lane, lane - 40) % 3
    a1, a2, a3 = coeffs
    right = a3 * diff
    right += jnp.where(place >= 1, a2, 0.0) * pltpu.roll(diff, 1, 1)
    right += jnp.where(place >= 2, a1, 0.0) * pltpu.roll(diff, 2, 1)
    left = a3 * diff
    left += jnp.where(place <= 1, a2, 0.0) * pltpu.roll(diff, COLS - 1, 1)
    left += jnp.where(place == 0, a1, 0.0) * pltpu.roll(diff, COLS - 2, 1)
    return jnp.where(low, right, -left)


def spread(packed, m, lane):
    a = jnp.where(lane >= 125, pltpu.roll(packed, 125 - 3 * m, 1), 0.0)
    return a + jnp.where(lane < 3, pltpu.roll(packed, 88 - 3 * m, 1), 0.0)


def sine(x):
    z = x * x
    poly = 1.0 / 6227020800.0
    for c in (-1.0 / 39916800.0, 1.0 / 362880.0, -1.0 / 5040.0, 1.0 / 120.0, -1.0 / 6.0):
        poly = poly * z + c
    return x + x * z * poly


def grid_block(i, j):
    summed = i + j
    summed = jnp.minimum(summed, 2 * LAST - summed).astype(jnp.float32)
    differ = (i - j).astype(jnp.float32)
    same = i == j
    denom = -2.0 * sine(HALF * summed) * sine(HALF * differ)
    safe = jnp.where(same, 1.0, denom)

    def edge(index):
        return (index == 0) | (index == LAST)

    ratio = jnp.where(edge(i), 2.0, 1.0) * jnp.where(edge(j), 0.5, 1.0)
    ratio = jnp.where((i + j) % 2 == 0, ratio, -ratio)
    wave = sine(HALF * jnp.minimum(2 * i, 2 * (LAST - i)).astype(jnp.float32))
    off = (math.pi / LAST) * wave * ratio / safe
    tall = jnp.where(edge(i), 1.0, wave)
    diagonal = -HALF * sine(HALF * (LAST - 2 * i).astype(jnp.float32)) / tall
    return jnp.where(same, jnp.where(edge(i), 0.0, diagonal), off).astype(jnp.bfloat16)


def kernel(
    rho_ref,
    speed_ref,
    temp_ref,
    shear_ref,
    heat_ref,
    own_ref,
    par_ref,
    U,
    R,
    F1,
    F2,
    enc,
    encr,
    acc,
    ps1,
    pr1,
    ps2,
    pr2,
    D,
    G,
    Go,
    GT,
    GTo,
    GT2,
    H,
    H2,
    TT,
    zs,
    z_s,
    z_r,
    a_s,
    a_r,
    h_s,
    h_r,
    p1_s,
    p1_r,
    f2_s,
    f2_r,
    g_s,
    g_r,
    p2_s,
    p2_r,
    o_s,
    o_r,
):
    gx = lax.axis_index("gx")
    gy = lax.axis_index("gy")
    gxn = lax.axis_size("gx")
    x = gy // 4
    s = (gy // 2) % 2
    c = gy % 2

    def at(dgx, xx, ss, cc):
        return ((gx + dgx + gxn) % gxn, xx * 4 + ss * 2 + cc)

    partner = at(0, x, 1 - s, c)
    sibling = at(0, x, s, 1 - c)
    peers = [at(0, (x + k) % 4, s, c) for k in (1, 2, 3)]
    left_to = at(s - 1, x, 1 - s, c)
    right_to = at(s, x, 1 - s, c)
    beside = at(1 - 2 * s, x, s, c)

    barrier = pltpu.get_barrier_semaphore()
    greet = [partner, sibling, *peers, at(2 * s - 1, x, 1 - s, c), at(1, x, s, c), at(-1, x, s, c)]
    for who in greet:
        pl.semaphore_signal(barrier, inc=1, device_id=who, device_id_type=MESH)

    mine = pl.multiple_of(s * COLS, COLS)
    other = pl.multiple_of((1 - s) * COLS, COLS)
    base = pl.multiple_of(s * ROWS, ROWS)
    pbase = pl.multiple_of((1 - s) * ROWS, ROWS)
    lane = lax.broadcasted_iota(jnp.int32, (TILE, COLS), 1)

    def remote(src, dst, ssem, rsem, who):
        return pltpu.make_async_remote_copy(
            src_ref=src, dst_ref=dst, send_sem=ssem, recv_sem=rsem, device_id=who, device_id_type=MESH
        )

    def inputs(r, col):
        rows, cols = pl.ds(r, TILE), pl.ds(col, COLS)
        u = [rho_ref[rows, cols]]
        u += [speed_ref[k, rows, cols] for k in range(3)]
        u.append(temp_ref[rows, cols])
        u += [shear_ref[k, rows, cols] for k in range(5)]
        u += [heat_ref[k, rows, cols] for k in range(3)]
        return u

    def wall_of(r):
        k = r + lax.broadcasted_iota(jnp.int32, (TILE, COLS), 0)
        row = x * 256 + (r // ROWS) * 128 + c * ROWS + (k - (r // ROWS) * ROWS)
        return jnp.where(row == 0, 1.0, jnp.where(row == LAST, -1.0, 0.0))

    @pl.loop(0, ROWS // TILE)
    def _(t):
        r = pl.multiple_of(t * TILE, TILE)
        u = inputs(r, other)
        for m in range(FIELDS):
            enc[m, pl.ds(r, TILE), :] = encode(u[m], m)
        Go[pl.ds(base + r, TILE), :] = edges(flux(u, 0), lane)
        G[pl.ds(pbase + r, TILE), :] = jnp.zeros((TILE, COLS), jnp.float32)
        Go[pl.ds(pbase + r, TILE), :] = jnp.zeros((TILE, COLS), jnp.float32)

    def first(r, u, side, k):
        rows = pl.ds(r, TILE)
        fy = flux(u, 1)
        for m in range(FIELDS):
            U[m, rows, :] = u[m]
            F1[m, side, x, pl.ds(k, TILE), :] = fy[m].astype(jnp.bfloat16)
        fx = flux(u, 0)
        G[rows, :] = edges(fx, lane)
        src = source(u, wall_of(r))
        for m in range(FIELDS):
            along = stencil(fx[m])
            R[m, rows, :] = -along if src[m] is None else src[m] - along

    @pl.loop(0, ROWS // TILE)
    def _(t):
        r = pl.multiple_of(t * TILE, TILE)
        first(pl.multiple_of(base + r, TILE), inputs(r, mine), s, r)

    GT[...] = G[...].T
    GTo[...] = Go[...].T
    H[s, s] = GTo[pl.ds(pl.multiple_of(40 * s, 8), 40), :]

    pl.semaphore_wait(barrier, len(greet))

    low, high = pl.ds(0, 40), pl.ds(40, 40)
    halos = [
        remote(GT.at[low], H.at[0, s], h_s.at[0], h_r.at[0], left_to),
        remote(GT.at[high], H.at[1, s], h_s.at[1], h_r.at[1], right_to),
        remote(
            GTo.at[pl.ds(pl.multiple_of(40 * (1 - s), 8), 40)],
            H.at[1 - s, s],
            h_s.at[2],
            h_r.at[2],
            beside,
        ),
    ]
    for copy in halos:
        copy.start()

    step = ROWS // PARTS

    def swap(t):
        rows = pl.ds(pl.multiple_of(t * step, step), step)
        return remote(enc.at[:, rows], encr.at[:, rows], z_s.at[t], z_r.at[t], partner)

    for t in range(PARTS):
        swap(t).start()

    def gather_own(k):
        block = F1.at[:, s, x]
        return remote(block, block, a_s.at[PARTS, k], a_r.at[PARTS, k], peers[k])

    def gather_part(t, k):
        block = F1.at[:, 1 - s, x, pl.ds(pl.multiple_of(t * step, step), step)]
        return remote(block, block, a_s.at[t, k], a_r.at[t, k], peers[k])

    for k in range(3):
        gather_own(k).start()

    @pl.loop(0, 256 // TILE)
    def _(t):
        p = pl.multiple_of(t * TILE, TILE)
        row = p + lax.broadcasted_iota(jnp.int32, (TILE, 512), 0)
        rr = row % 128
        core = jnp.where(row < 128, c, 1 - c)
        i = x * 256 + (rr // ROWS) * 128 + core * ROWS + rr % ROWS
        col = lax.broadcasted_iota(jnp.int32, (TILE, 512), 1)
        j = ((col % 256) // ROWS) * 256 + (col // 256) * 128 + c * ROWS + col % ROWS
        D[pl.ds(p, TILE), :] = grid_block(i, j)

    for k in range(3):
        gather_own(k).wait_recv()

    def product(side, m):
        columns = pl.ds(pl.multiple_of(side * 256, 256), 256)
        block = F1[m, side].reshape(256, COLS)
        return jnp.dot(D[:, columns], block, preferred_element_type=jnp.float32)

    @pl.loop(0, FIELDS)
    def _(m):
        acc[m] = product(s, m)

    @pl.loop(0, PARTS)
    def _(t):
        swap(t).wait_recv()

        @pl.loop(0, step // TILE)
        def _(v):
            k = pl.multiple_of(t * step + v * TILE, TILE)
            u = [decode(encr[m, pl.ds(k, TILE), :], m) for m in range(FIELDS)]
            first(pl.multiple_of(pbase + k, TILE), u, 1 - s, k)

        for k in range(3):
            gather_part(t, k).start()

    @pl.loop(0, PARTS)
    def _(t):
        for k in range(3):
            gather_part(t, k).wait_recv()

    def share1(m):
        return remote(ps1.at[m], pr1.at[m], p1_s.at[m], p1_r.at[m], sibling)

    @pl.loop(0, FIELDS)
    def _(m):
        total = acc[m] + product(1 - s, m)
        ps1[m] = total[128:]
        acc[m, pl.ds(0, 128)] = total[:128]
        share1(m).start()

    def packed(rows, right, left):
        TT[pl.ds(0, 40), :] = right
        TT[pl.ds(40, 40), :] = left
        TT[pl.ds(80, 48), :] = jnp.zeros((48, COLS), jnp.float32)
        TT[...] = TT[...].T

    for copy in halos:
        copy.wait_recv()
    packed(None, H[0, 0] + H[0, 1], H[1, 0] + H[1, 1])

    @pl.loop(0, FIELDS)
    def _(m):
        share1(m).wait_recv()

    @pl.loop(0, 128 // TILE)
    def _(t):
        r = pl.multiple_of(t * TILE, TILE)
        rows = pl.ds(r, TILE)
        edge = mend(TT[rows, :] - G[rows, :], lane)
        u, rate = [], []
        for m in range(FIELDS):
            one = R[m, rows, :] - spread(edge, m, lane) - (acc[m, rows, :] + pr1[m, rows, :])
            rate.append(one)
            u.append(U[m, rows, :] + time_step * one)
        fy = flux(u, 1)
        side = r // ROWS
        k = pl.multiple_of(r - side * ROWS, TILE)
        for m in range(FIELDS):
            F2[m, side, x, pl.ds(k, TILE), :] = fy[m].astype(jnp.bfloat16)
        fx = flux(u, 0)
        G[rows, :] = edges(fx, lane)
        src = source(u, wall_of(r))
        for m in range(FIELDS):
            two = rate[m] - stencil(fx[m])
            R[m, rows, :] = 0.5 * (two if src[m] is None else two + src[m])

    def gather2(m, k):
        block = F2.at[m, :, x]
        return remote(block, block, f2_s.at[m, k], f2_r.at[m, k], peers[k])

    GT2[...] = G[...].T
    halos2 = [
        remote(GT2.at[low], H2.at[0], g_s.at[0], g_r.at[0], left_to),
        remote(GT2.at[high], H2.at[1], g_s.at[1], g_r.at[1], right_to),
    ]
    for copy in halos2:
        copy.start()

    @pl.loop(0, FIELDS)
    def _(m):
        for k in range(3):
            gather2(m, k).start()

    def share2(m):
        return remote(ps2.at[m], pr2.at[m], p2_s.at[m], p2_r.at[m], sibling)

    def give(m):
        return remote(zs.at[m], par_ref.at[m], o_s.at[m], o_r.at[m], partner)

    def front(m):
        for k in range(3):
            gather2(m, k).wait_recv()
        total = jnp.dot(D[...], F2[m].reshape(512, COLS), preferred_element_type=jnp.float32)
        ps2[m] = total[128:]
        acc[m, pl.ds(0, 128)] = total[:128]
        share2(m).start()

    def back(m):
        share2(m).wait_recv()

        def value(first_row):
            rows = pl.ds(first_row, ROWS)
            return R[m, rows, :] - 0.5 * (acc[m, rows, :] + pr2[m, rows, :])

        zs[m] = value(pbase).astype(jnp.bfloat16)
        give(m).start()
        own_ref[m] = value(base)

    @pl.loop(0, LAG)
    def _(m):
        front(m)

    for copy in halos2:
        copy.wait_recv()
    packed(None, H2[0], H2[1])

    @pl.loop(0, 128 // TILE)
    def _(t):
        rows = pl.ds(pl.multiple_of(t * TILE, TILE), TILE)
        edge = 0.5 * mend(TT[rows, :] - G[rows, :], lane)
        for m in range(FIELDS):
            R[m, rows, :] = R[m, rows, :] - spread(edge, m, lane)

    @pl.loop(LAG, FIELDS)
    def _(m):
        front(m)
        back(m - LAG)

    @pl.loop(FIELDS - LAG, FIELDS)
    def _(m):
        back(m)

    for copy in halos + halos2:
        copy.wait_send()
    for k in range(3):
        gather_own(k).wait_send()

    @pl.loop(0, PARTS)
    def _(t):
        swap(t).wait_send()
        for k in range(3):
            gather_part(t, k).wait_send()

    @pl.loop(0, FIELDS)
    def _(m):
        share1(m).wait_send()
        share2(m).wait_send()
        for k in range(3):
            gather2(m, k).wait_send()
        give(m).wait_send()

    @pl.loop(0, FIELDS)
    def _(m):
        give(m).wait_recv()


def on_device(mass_per_volume, motion_speed, agitation_energy, shear_deviatoric, thermal_current_array):
    def moved(a):
        return jnp.transpose(a, (1, 0, 2))

    full = (FIELDS, 128, COLS)
    gathered = (FIELDS, 2, 4, ROWS, COLS)
    dma = pltpu.SemaphoreType.DMA
    f32, bf16 = jnp.float32, jnp.bfloat16
    own, par = pl.pallas_call(
        kernel,
        out_shape=(
            jax.ShapeDtypeStruct((FIELDS, ROWS, COLS), f32),
            jax.ShapeDtypeStruct((FIELDS, ROWS, COLS), bf16),
        ),
        in_specs=[pl.BlockSpec(memory_space=pltpu.VMEM)] * 5,
        out_specs=(pl.BlockSpec(memory_space=pltpu.VMEM),) * 2,
        scratch_shapes=[
            pltpu.VMEM(full, f32),
            pltpu.VMEM(full, f32),
            pltpu.VMEM(gathered, bf16),
            pltpu.VMEM(gathered, bf16),
            pltpu.VMEM((FIELDS, ROWS, COLS), bf16),
            pltpu.VMEM((FIELDS, ROWS, COLS), bf16),
            pltpu.VMEM((FIELDS, 256, COLS), f32),
            pltpu.VMEM(full, f32),
            pltpu.VMEM(full, f32),
            pltpu.VMEM(full, f32),
            pltpu.VMEM(full, f32),
            pltpu.VMEM((256, 512), bf16),
            pltpu.VMEM((128, COLS), f32),
            pltpu.VMEM((128, COLS), f32),
            pltpu.VMEM((COLS, 128), f32),
            pltpu.VMEM((COLS, 128), f32),
            pltpu.VMEM((COLS, 128), f32),
            pltpu.VMEM((2, 2, 40, 128), f32),
            pltpu.VMEM((2, 40, 128), f32),
            pltpu.VMEM((128, 128), f32),
            pltpu.VMEM((FIELDS, ROWS, COLS), bf16),
            dma((PARTS,)),
            dma((PARTS,)),
            dma((PARTS + 1, 3)),
            dma((PARTS + 1, 3)),
            dma((3,)),
            dma((3,)),
            dma((FIELDS,)),
            dma((FIELDS,)),
            dma((FIELDS, 3)),
            dma((FIELDS, 3)),
            dma((2,)),
            dma((2,)),
            dma((FIELDS,)),
            dma((FIELDS,)),
            dma((FIELDS,)),
            dma((FIELDS,)),
        ],
        compiler_params=pltpu.CompilerParams(
            collective_id=0, has_side_effects=True, vmem_limit_bytes=40 * 1024 * 1024
        ),
        name="sections",
    )(
        mass_per_volume,
        moved(motion_speed),
        agitation_energy,
        moved(shear_deviatoric),
        moved(thermal_current_array),
    )
    par = par.astype(f32)
    lower = (lax.axis_index("gy") // 2) % 2 == 0
    halves = [jnp.where(lower, own, par), jnp.where(lower, par, own)]
    return jnp.transpose(jnp.concatenate(halves, axis=2), (1, 0, 2))


def solution(mesh):
    return jax.shard_map(
        on_device,
        mesh=mesh,
        in_specs=(
            P("gy", "gx"),
            P("gy", None, "gx"),
            P("gy", "gx"),
            P("gy", None, "gx"),
            P("gy", None, "gx"),
        ),
        out_specs=P("gy", None, "gx"),
        check_vma=False,
    )
```

time: 400 us -> 95.6 us (0.24); the launches traced: 395 us -> 95.3 us
  waiting for transfers between devices: 280 us -> 0 us
  Pallas kernels: 0 us -> 89.7 us
  starting transfers between devices: 29.8 us -> 0 us
  other arithmetic: 26.3 us -> 1.06 us
  matrix products: 21.5 us -> 0 us
  local copies, waits for them, and re-layouts: 23.5 us -> 4.5 us
  between operations: 14 us -> 0.02 us
    all_gather x2 -> x0, waiting for transfers between devices: 280 us -> none  [wall_normal(): piece = lax.all_gather(lowered, 'gy', axis=0, tiled=True)]
    pallas_call x0 -> x1, Pallas kernels: none -> 89.7 us  [on_device(): pl.pallas_call(kernel, out_shape=(jax.ShapeDtypeStruct((FIELDS, ROWS, COL...]
    ppermute x4 -> x0, starting transfers between devices: 29.7 us -> none  [the longest x2 25.7 us: extended(): after = lax.ppermute(initial, axis, down)]
    unnamed x60 -> x0, other arithmetic: 23 us -> none
    dot_general x2 -> x0, matrix products: 21.5 us -> none  [wall_normal(): jnp.dot(grid, piece.reshape(piece.shape[0], -1), preferred_element_type=j...]
    all_gather x2 -> x0, local copies, waits for them, and re-layouts: 20.6 us -> none  [wall_normal(): piece = lax.all_gather(lowered, 'gy', axis=0, tiled=True)]
  transfers between devices with their start and end apart: 6 -> 0, of which waited for: 2 -> 0; matrix products, arithmetic and copies ran while one was open for 9% -> 0% of each run, Pallas kernels for 0% -> 0%
where the time goes in v1:
time: 95.6 us; the launch traced here: 95.3 us
  Pallas kernels  89.7 us (94%)
  local copies, waits for them, and re-layouts  4.5 us (5%)
  other arithmetic  1.06 us (1%)
    pallas_call x1, Pallas kernels, on_device(): pl.pallas_call(kernel, out_shape=(jax.ShapeDtypeStruct((FIELDS, ROWS, COL...  89.7 us
    unnamed x10, local copies, waits for them, and re-layouts  4.5 us

profile of v1, /device:TPU:1, one launch (start us, length us, event | category | flops | bytes accessed | tf_op | source)
XLA Modules:
  0.0 95.3 jit_solution(4495096996561675215)
XLA Ops:
  0.0 0.0 copy-start
  0.0 1.0 %copy-done = f32[64,5,256]{2,0,1:T(8,128)S(1)} copy-done((f32[64,5,256]{2,0,1:T(8,128)S(1)}, f32[64,5,256]{2,0,1:T(8,128)}, u32[]{:S(2)}) %copy-start) | copy-done | bytes 327704
  1.0 0.0 copy-start.1
  1.0 0.9 copy-done.1
  1.9 0.0 copy-start.2
  1.9 0.9 copy-done.2
  2.8 0.0 copy-start.3
  2.8 0.8 copy-done.3
  3.7 0.0 copy-start.4
  3.7 0.8 copy-done.4
  4.5 89.7 %sections.1 = (f32[13,64,128]{2,1,0:T(8,128)S(1)}, bf16[13,64,128]{2,1,0:T(8,128)(2,1)S(1)}) custom-call(f32[64,256]{1,0:T(8,128)S(1)} %copy-done.3, f32[3,64,256]{2,1,0:T(8,128)S(1)} %bitcast.6, f32[64,256]{1,0:T(8,128)S(1)} %copy-done.4, f32[5,64,256]{2,1,0:T(8,128)S(1)} %bitcast.5, f32[3,64,256]{2,1,0:T(8,128)S(1)} %bitcast.7), custom_call_target="tpu_custom_call" | custom-call | tf_op jit(solution)/shard_map/sections/pallas_call | solution.py:490
  94.2 0.1 convert_select_fusion.1
  94.3 1.0 %maximum_bitcast_fusion = f32[64,13,256]{2,0,1:T(8,128)} fusion(f32[13,64,128]{2,1,0:T(8,128)S(1)} %get-tuple-element.10, f32[13,64,128]{2,1,0:T(8,128)S(1)} %get-tuple-element.9), kind=kLoop, calls=%fused_computation | loop fusion | flops 212992 | bytes 1703936 | tf_op jit(solution)/shard_map/transpose | solution.py:551
Async XLA Ops:
  0.0 1.0 %copy-start = (f32[64,5,256]{2,0,1:T(8,128)S(1)}, f32[64,5,256]{2,0,1:T(8,128)}, u32[]{:S(2)}) copy-start(f32[64,5,256]{2,0,1:T(8,128)} %param.8) | copy-start | bytes 983044
  1.0 0.9 copy-start.1
  1.9 0.9 copy-start.2
  2.8 0.8 copy-start.3
  3.7 0.8 copy-start.4

commit v2 on v1

--- a/solution.py
+++ b/solution.py
@@ -161,14 +161,14 @@
     pr2,
     D,
     G,
-    Go,
-    GT,
-    GTo,
+    GT1,
     GT2,
-    H,
+    H1,
     H2,
     TT,
+    X,
     zs,
+    in_s,
     z_s,
     z_r,
     a_s,
@@ -201,10 +201,9 @@
     peers = [at(0, (x + k) % 4, s, c) for k in (1, 2, 3)]
     left_to = at(s - 1, x, 1 - s, c)
     right_to = at(s, x, 1 - s, c)
-    beside = at(1 - 2 * s, x, s, c)
 
     barrier = pltpu.get_barrier_semaphore()
-    greet = [partner, sibling, *peers, at(2 * s - 1, x, 1 - s, c), at(1, x, s, c), at(-1, x, s, c)]
+    greet = [partner, sibling, *peers, at(2 * s - 1, x, 1 - s, c)]
     for who in greet:
         pl.semaphore_signal(barrier, inc=1, device_id=who, device_id_type=MESH)
 
@@ -219,29 +218,48 @@
             src_ref=src, dst_ref=dst, send_sem=ssem, recv_sem=rsem, device_id=who, device_id_type=MESH
         )
 
-    def inputs(r, col):
-        rows, cols = pl.ds(r, TILE), pl.ds(col, COLS)
-        u = [rho_ref[rows, cols]]
-        u += [speed_ref[k, rows, cols] for k in range(3)]
-        u.append(temp_ref[rows, cols])
-        u += [shear_ref[k, rows, cols] for k in range(5)]
-        u += [heat_ref[k, rows, cols] for k in range(3)]
-        return u
+    def load(half, column):
+        cols = pl.ds(column, COLS)
+        groups = ((rho_ref, 0, 0), (speed_ref, 1, 3), (temp_ref, 4, 0), (shear_ref, 5, 5), (heat_ref, 10, 3))
+        copies = []
+        for n, (ref, start, count) in enumerate(groups):
+            src = ref.at[:, :, cols] if count else ref.at[:, cols]
+            dst = X.at[half, pl.ds(start, count)] if count else X.at[half, start]
+            copies.append(pltpu.make_async_copy(src, dst, in_s.at[half, n]))
+        return copies
+
+    loads = [load(0, other), load(1, mine)]
+    for copy in loads[0] + loads[1]:
+        copy.start()
+
+    def inputs(half, r):
+        return [X[half, m, pl.ds(r, TILE), :] for m in range(FIELDS)]
 
     def wall_of(r):
         k = r + lax.broadcasted_iota(jnp.int32, (TILE, COLS), 0)
         row = x * 256 + (r // ROWS) * 128 + c * ROWS + (k - (r // ROWS) * ROWS)
         return jnp.where(row == 0, 1.0, jnp.where(row == LAST, -1.0, 0.0))
 
+    for copy in loads[0]:
+        copy.wait()
+
     @pl.loop(0, ROWS // TILE)
     def _(t):
         r = pl.multiple_of(t * TILE, TILE)
-        u = inputs(r, other)
+        u = inputs(0, r)
         for m in range(FIELDS):
             enc[m, pl.ds(r, TILE), :] = encode(u[m], m)
-        Go[pl.ds(base + r, TILE), :] = edges(flux(u, 0), lane)
-        G[pl.ds(pbase + r, TILE), :] = jnp.zeros((TILE, COLS), jnp.float32)
-        Go[pl.ds(pbase + r, TILE), :] = jnp.zeros((TILE, COLS), jnp.float32)
+
+    pl.semaphore_wait(barrier, len(greet))
+
+    step = ROWS // PARTS
+
+    def swap(t):
+        rows = pl.ds(pl.multiple_of(t * step, step), step)
+        return remote(enc.at[:, rows], encr.at[:, rows], z_s.at[t], z_r.at[t], partner)
+
+    for t in range(PARTS):
+        swap(t).start()
 
     def first(r, u, side, k):
         rows = pl.ds(r, TILE)
@@ -256,40 +274,13 @@
             along = stencil(fx[m])
             R[m, rows, :] = -along if src[m] is None else src[m] - along
 
+    for copy in loads[1]:
+        copy.wait()
+
     @pl.loop(0, ROWS // TILE)
     def _(t):
         r = pl.multiple_of(t * TILE, TILE)
-        first(pl.multiple_of(base + r, TILE), inputs(r, mine), s, r)
-
-    GT[...] = G[...].T
-    GTo[...] = Go[...].T
-    H[s, s] = GTo[pl.ds(pl.multiple_of(40 * s, 8), 40), :]
-
-    pl.semaphore_wait(barrier, len(greet))
-
-    low, high = pl.ds(0, 40), pl.ds(40, 40)
-    halos = [
-        remote(GT.at[low], H.at[0, s], h_s.at[0], h_r.at[0], left_to),
-        remote(GT.at[high], H.at[1, s], h_s.at[1], h_r.at[1], right_to),
-        remote(
-            GTo.at[pl.ds(pl.multiple_of(40 * (1 - s), 8), 40)],
-            H.at[1 - s, s],
-            h_s.at[2],
-            h_r.at[2],
-            beside,
-        ),
-    ]
-    for copy in halos:
-        copy.start()
-
-    step = ROWS // PARTS
-
-    def swap(t):
-        rows = pl.ds(pl.multiple_of(t * step, step), step)
-        return remote(enc.at[:, rows], encr.at[:, rows], z_s.at[t], z_r.at[t], partner)
-
-    for t in range(PARTS):
-        swap(t).start()
+        first(pl.multiple_of(base + r, TILE), inputs(1, r), s, r)
 
     def gather_own(k):
         block = F1.at[:, s, x]
@@ -316,14 +307,25 @@
     for k in range(3):
         gather_own(k).wait_recv()
 
-    def product(side, m):
+    def product(side, fields):
         columns = pl.ds(pl.multiple_of(side * 256, 256), 256)
-        block = F1[m, side].reshape(256, COLS)
-        return jnp.dot(D[:, columns], block, preferred_element_type=jnp.float32)
-
-    @pl.loop(0, FIELDS)
-    def _(m):
-        acc[m] = product(s, m)
+        blocks = [F1[m, side].reshape(256, COLS) for m in fields]
+        block = jnp.concatenate(blocks, axis=1) if len(blocks) > 1 else blocks[0]
+        total = jnp.dot(D[:, columns], block, preferred_element_type=jnp.float32)
+        return [total[:, n * COLS : (n + 1) * COLS] for n in range(len(blocks))]
+
+    def in_pairs(body):
+        @pl.loop(0, FIELDS // 2)
+        def _(p):
+            body((2 * p, 2 * p + 1))
+
+        body((FIELDS - 1,))
+
+    def own_side(fields):
+        for m, total in zip(fields, product(s, fields)):
+            acc[m] = total
+
+    in_pairs(own_side)
 
     @pl.loop(0, PARTS)
     def _(t):
@@ -338,6 +340,20 @@
         for k in range(3):
             gather_part(t, k).start()
 
+    low, high = pl.ds(0, 40), pl.ds(40, 40)
+
+    def send_edges(GT, H, ssem, rsem):
+        GT[...] = G[...].T
+        copies = [
+            remote(GT.at[low], H.at[0], ssem.at[0], rsem.at[0], left_to),
+            remote(GT.at[high], H.at[1], ssem.at[1], rsem.at[1], right_to),
+        ]
+        for copy in copies:
+            copy.start()
+        return copies
+
+    halos1 = send_edges(GT1, H1, h_s, h_r)
+
     @pl.loop(0, PARTS)
     def _(t):
         for k in range(3):
@@ -346,22 +362,23 @@
     def share1(m):
         return remote(ps1.at[m], pr1.at[m], p1_s.at[m], p1_r.at[m], sibling)
 
-    @pl.loop(0, FIELDS)
-    def _(m):
-        total = acc[m] + product(1 - s, m)
-        ps1[m] = total[128:]
-        acc[m, pl.ds(0, 128)] = total[:128]
-        share1(m).start()
-
-    def packed(rows, right, left):
-        TT[pl.ds(0, 40), :] = right
-        TT[pl.ds(40, 40), :] = left
+    def other_side(fields):
+        for m, total in zip(fields, product(1 - s, fields)):
+            ps1[m] = acc[m, pl.ds(128, 128)] + total[128:]
+            share1(m).start()
+            acc[m, pl.ds(0, 128)] += total[:128]
+
+    in_pairs(other_side)
+
+    def receive_edges(copies, H):
+        for copy in copies:
+            copy.wait_recv()
+        TT[low, :] = H[0]
+        TT[high, :] = H[1]
         TT[pl.ds(80, 48), :] = jnp.zeros((48, COLS), jnp.float32)
         TT[...] = TT[...].T
 
-    for copy in halos:
-        copy.wait_recv()
-    packed(None, H[0, 0] + H[0, 1], H[1, 0] + H[1, 1])
+    receive_edges(halos1, H1)
 
     @pl.loop(0, FIELDS)
     def _(m):
@@ -393,18 +410,12 @@
         block = F2.at[m, :, x]
         return remote(block, block, f2_s.at[m, k], f2_r.at[m, k], peers[k])
 
-    GT2[...] = G[...].T
-    halos2 = [
-        remote(GT2.at[low], H2.at[0], g_s.at[0], g_r.at[0], left_to),
-        remote(GT2.at[high], H2.at[1], g_s.at[1], g_r.at[1], right_to),
-    ]
-    for copy in halos2:
-        copy.start()
-
     @pl.loop(0, FIELDS)
     def _(m):
         for k in range(3):
             gather2(m, k).start()
+
+    halos2 = send_edges(GT2, H2, g_s, g_r)
 
     def share2(m):
         return remote(ps2.at[m], pr2.at[m], p2_s.at[m], p2_r.at[m], sibling)
@@ -435,9 +446,7 @@
     def _(m):
         front(m)
 
-    for copy in halos2:
-        copy.wait_recv()
-    packed(None, H2[0], H2[1])
+    receive_edges(halos2, H2)
 
     @pl.loop(0, 128 // TILE)
     def _(t):
@@ -455,7 +464,7 @@
     def _(m):
         back(m)
 
-    for copy in halos + halos2:
+    for copy in halos1 + halos2:
         copy.wait_send()
     for k in range(3):
         gather_own(k).wait_send()
@@ -493,7 +502,7 @@
             jax.ShapeDtypeStruct((FIELDS, ROWS, COLS), f32),
             jax.ShapeDtypeStruct((FIELDS, ROWS, COLS), bf16),
         ),
-        in_specs=[pl.BlockSpec(memory_space=pltpu.VMEM)] * 5,
+        in_specs=[pl.BlockSpec(memory_space=pltpu.HBM)] * 5,
         out_specs=(pl.BlockSpec(memory_space=pltpu.VMEM),) * 2,
         scratch_shapes=[
             pltpu.VMEM(full, f32),
@@ -509,20 +518,20 @@
             pltpu.VMEM(full, f32),
             pltpu.VMEM((256, 512), bf16),
             pltpu.VMEM((128, COLS), f32),
-            pltpu.VMEM((128, COLS), f32),
             pltpu.VMEM((COLS, 128), f32),
             pltpu.VMEM((COLS, 128), f32),
-            pltpu.VMEM((COLS, 128), f32),
-            pltpu.VMEM((2, 2, 40, 128), f32),
+            pltpu.VMEM((2, 40, 128), f32),
             pltpu.VMEM((2, 40, 128), f32),
             pltpu.VMEM((128, 128), f32),
+            pltpu.VMEM((2, FIELDS, ROWS, COLS), f32),
             pltpu.VMEM((FIELDS, ROWS, COLS), bf16),
+            dma((2, 5)),
             dma((PARTS,)),
             dma((PARTS,)),
             dma((PARTS + 1, 3)),
             dma((PARTS + 1, 3)),
-            dma((3,)),
-            dma((3,)),
+            dma((2,)),
+            dma((2,)),
             dma((FIELDS,)),
             dma((FIELDS,)),
             dma((FIELDS, 3)),
@@ -535,7 +544,7 @@
             dma((FIELDS,)),
         ],
         compiler_params=pltpu.CompilerParams(
-            collective_id=0, has_side_effects=True, vmem_limit_bytes=40 * 1024 * 1024
+            collective_id=0, has_side_effects=True, vmem_limit_bytes=66_500_000
         ),
         name="sections",
     )(

time: 95.6 us -> 85.4 us (0.89); the launches traced: 95.3 us -> 84.1 us
  Pallas kernels: 89.7 us -> 82 us
  local copies, waits for them, and re-layouts: 4.5 us -> 0 us
  other arithmetic: 1.06 us -> 2.12 us
    pallas_call x1, Pallas kernels: 89.7 us -> 82 us  [on_device(): pl.pallas_call(kernel, out_shape=(jax.ShapeDtypeStruct((FIELDS, ROWS, COL...]
    unnamed x10 -> x0, local copies, waits for them, and re-layouts: 4.5 us -> none
    select_n x1, other arithmetic: 0.09 us -> 1.15 us  [on_device(): halves = [jnp.where(lower, own, par), jnp.where(lower, par, own)]]
where the time goes in v2:
time: 85.4 us; the launch traced here: 84.1 us
  Pallas kernels  82 us (96%)
  other arithmetic  2.12 us (2%)
    pallas_call x1, Pallas kernels, on_device(): pl.pallas_call(kernel, out_shape=(jax.ShapeDtypeStruct((FIELDS, ROWS, COL...  82 us

profile of v2, /device:TPU:1, one launch (start us, length us, event | category | flops | bytes accessed | tf_op | source)
XLA Modules:
  0.0 84.1 jit_solution(9667653557084380332)
XLA Ops:
  0.0 82.0 %sections.1 = (f32[13,64,128]{2,1,0:T(8,128)}, bf16[13,64,128]{2,1,0:T(8,128)(2,1)}) custom-call(f32[64,256]{1,0:T(8,128)} %rho_ref.1, f32[3,64,256]{2,1,0:T(8,128)} %bitcast.6, f32[64,256]{1,0:T(8,128)} %temp_ref.1, f32[5,64,256]{2,1,0:T(8,128)} %bitcast.5, f32[3,64,256]{2,1,0:T(8,128)} %bitcast.7), custom_call_target="tpu_custom_call" | custom-call | tf_op jit(solution)/shard_map/sections/pallas_call | solution.py:499
  82.0 1.2 %convert_select_fusion.1 = (f32[13,64,128]{2,1,0:T(8,128)S(1)}, f32[13,64,128]{2,1,0:T(8,128)S(1)}) fusion(f32[13,64,128]{2,1,0:T(8,128)} %get-tuple-element.7, bf16[13,64,128]{2,1,0:T(8,128)(2,1)} %get-tuple-element.8, pred[]{:T(512)S(6)} %eq.5), kind=kLoop, calls=%fused_computation.2 | loop fusion | flops 319488 | bytes 1490945 | tf_op jit(solution)/shard_map/jit(_where)/select_n | solution.py:559
  83.1 1.0 %maximum_bitcast_fusion = f32[64,13,256]{2,0,1:T(8,128)} fusion(f32[13,64,128]{2,1,0:T(8,128)S(1)} %get-tuple-element.10, f32[13,64,128]{2,1,0:T(8,128)S(1)} %get-tuple-element.9), kind=kLoop, calls=%fused_computation | loop fusion | flops 212992 | bytes 1703936 | tf_op jit(solution)/shard_map/transpose | solution.py:560

commit v3 on v2

--- a/solution.py
+++ b/solution.py
@@ -22,8 +22,8 @@
 ROWS = 64
 COLS = 128
 TILE = 16
-PARTS = 4
-LAG = 2
+PARTS = ROWS // TILE
+LEAD = 3
 
 SPREAD = [(160.0, 1.25)] + [(40.0, 0.0)] * 3 + [(160.0, 1.25)] + [(50.0, 0.0)] * 8
 
@@ -146,9 +146,10 @@
     temp_ref,
     shear_ref,
     heat_ref,
-    own_ref,
-    par_ref,
+    OUT,
+    par,
     U,
+    FX,
     R,
     F1,
     F2,
@@ -252,21 +253,22 @@
 
     pl.semaphore_wait(barrier, len(greet))
 
-    step = ROWS // PARTS
-
     def swap(t):
-        rows = pl.ds(pl.multiple_of(t * step, step), step)
+        rows = pl.ds(pl.multiple_of(t * TILE, TILE), TILE)
         return remote(enc.at[:, rows], encr.at[:, rows], z_s.at[t], z_r.at[t], partner)
 
     for t in range(PARTS):
         swap(t).start()
 
-    def first(r, u, side, k):
+    def across_flux(F, u, side, k):
+        fy = flux(u, 1)
+        for m in range(FIELDS):
+            F[m, side, x, pl.ds(k, TILE), :] = fy[m].astype(jnp.bfloat16)
+
+    def first(r, u):
         rows = pl.ds(r, TILE)
-        fy = flux(u, 1)
         for m in range(FIELDS):
             U[m, rows, :] = u[m]
-            F1[m, side, x, pl.ds(k, TILE), :] = fy[m].astype(jnp.bfloat16)
         fx = flux(u, 0)
         G[rows, :] = edges(fx, lane)
         src = source(u, wall_of(r))
@@ -280,14 +282,16 @@
     @pl.loop(0, ROWS // TILE)
     def _(t):
         r = pl.multiple_of(t * TILE, TILE)
-        first(pl.multiple_of(base + r, TILE), inputs(1, r), s, r)
+        u = inputs(1, r)
+        across_flux(F1, u, s, r)
+        first(pl.multiple_of(base + r, TILE), u)
 
     def gather_own(k):
         block = F1.at[:, s, x]
         return remote(block, block, a_s.at[PARTS, k], a_r.at[PARTS, k], peers[k])
 
     def gather_part(t, k):
-        block = F1.at[:, 1 - s, x, pl.ds(pl.multiple_of(t * step, step), step)]
+        block = F1.at[:, 1 - s, x, pl.ds(pl.multiple_of(t * TILE, TILE), TILE)]
         return remote(block, block, a_s.at[t, k], a_r.at[t, k], peers[k])
 
     for k in range(3):
@@ -330,15 +334,12 @@
     @pl.loop(0, PARTS)
     def _(t):
         swap(t).wait_recv()
-
-        @pl.loop(0, step // TILE)
-        def _(v):
-            k = pl.multiple_of(t * step + v * TILE, TILE)
-            u = [decode(encr[m, pl.ds(k, TILE), :], m) for m in range(FIELDS)]
-            first(pl.multiple_of(pbase + k, TILE), u, 1 - s, k)
-
+        r = pl.multiple_of(t * TILE, TILE)
+        u = [decode(encr[m, pl.ds(r, TILE), :], m) for m in range(FIELDS)]
+        across_flux(F1, u, 1 - s, r)
         for k in range(3):
             gather_part(t, k).start()
+        first(pl.multiple_of(pbase + r, TILE), u)
 
     low, high = pl.ds(0, 40), pl.ds(40, 40)
 
@@ -389,39 +390,44 @@
         r = pl.multiple_of(t * TILE, TILE)
         rows = pl.ds(r, TILE)
         edge = mend(TT[rows, :] - G[rows, :], lane)
-        u, rate = [], []
+        u = []
         for m in range(FIELDS):
             one = R[m, rows, :] - spread(edge, m, lane) - (acc[m, rows, :] + pr1[m, rows, :])
-            rate.append(one)
+            R[m, rows, :] = one
             u.append(U[m, rows, :] + time_step * one)
-        fy = flux(u, 1)
+            U[m, rows, :] = u[m]
         side = r // ROWS
-        k = pl.multiple_of(r - side * ROWS, TILE)
-        for m in range(FIELDS):
-            F2[m, side, x, pl.ds(k, TILE), :] = fy[m].astype(jnp.bfloat16)
+        across_flux(F2, u, side, pl.multiple_of(r - side * ROWS, TILE))
         fx = flux(u, 0)
+        for m in range(FIELDS):
+            FX[m, rows, :] = fx[m]
         G[rows, :] = edges(fx, lane)
-        src = source(u, wall_of(r))
-        for m in range(FIELDS):
-            two = rate[m] - stencil(fx[m])
-            R[m, rows, :] = 0.5 * (two if src[m] is None else two + src[m])
 
     def gather2(m, k):
         block = F2.at[m, :, x]
         return remote(block, block, f2_s.at[m, k], f2_r.at[m, k], peers[k])
 
+    halos2 = send_edges(GT2, H2, g_s, g_r)
+
     @pl.loop(0, FIELDS)
     def _(m):
         for k in range(3):
             gather2(m, k).start()
 
-    halos2 = send_edges(GT2, H2, g_s, g_r)
+    @pl.loop(0, 128 // TILE)
+    def _(t):
+        r = pl.multiple_of(t * TILE, TILE)
+        rows = pl.ds(r, TILE)
+        src = source([U[m, rows, :] for m in range(FIELDS)], wall_of(r))
+        for m in range(FIELDS):
+            two = R[m, rows, :] - stencil(FX[m, rows, :])
+            R[m, rows, :] = 0.5 * (two if src[m] is None else two + src[m])
 
     def share2(m):
         return remote(ps2.at[m], pr2.at[m], p2_s.at[m], p2_r.at[m], sibling)
 
     def give(m):
-        return remote(zs.at[m], par_ref.at[m], o_s.at[m], o_r.at[m], partner)
+        return remote(zs.at[m], par.at[m], o_s.at[m], o_r.at[m], partner)
 
     def front(m):
         for k in range(3):
@@ -436,13 +442,16 @@
 
         def value(first_row):
             rows = pl.ds(first_row, ROWS)
-            return R[m, rows, :] - 0.5 * (acc[m, rows, :] + pr2[m, rows, :])
+            edge = spread(TT[rows, :], m, wide)
+            return R[m, rows, :] - edge - 0.5 * (acc[m, rows, :] + pr2[m, rows, :])
 
         zs[m] = value(pbase).astype(jnp.bfloat16)
         give(m).start()
-        own_ref[m] = value(base)
-
-    @pl.loop(0, LAG)
+        OUT[m, :, pl.ds(mine, COLS)] = value(base)
+
+    wide = lax.broadcasted_iota(jnp.int32, (ROWS, COLS), 1)
+
+    @pl.loop(0, LEAD)
     def _(m):
         front(m)
 
@@ -451,18 +460,23 @@
     @pl.loop(0, 128 // TILE)
     def _(t):
         rows = pl.ds(pl.multiple_of(t * TILE, TILE), TILE)
-        edge = 0.5 * mend(TT[rows, :] - G[rows, :], lane)
-        for m in range(FIELDS):
-            R[m, rows, :] = R[m, rows, :] - spread(edge, m, lane)
-
-    @pl.loop(LAG, FIELDS)
+        TT[rows, :] = 0.5 * mend(TT[rows, :] - G[rows, :], lane)
+
+    @pl.loop(0, LEAD - 1)
+    def _(m):
+        back(m)
+
+    @pl.loop(LEAD, FIELDS)
     def _(m):
         front(m)
-        back(m - LAG)
-
-    @pl.loop(FIELDS - LAG, FIELDS)
-    def _(m):
-        back(m)
+        back(m - 1)
+
+    back(FIELDS - 1)
+
+    @pl.loop(0, FIELDS)
+    def _(m):
+        give(m).wait_recv()
+        OUT[m, :, pl.ds(other, COLS)] = par[m].astype(jnp.float32)
 
     for copy in halos1 + halos2:
         copy.wait_send()
@@ -483,10 +497,6 @@
             gather2(m, k).wait_send()
         give(m).wait_send()
 
-    @pl.loop(0, FIELDS)
-    def _(m):
-        give(m).wait_recv()
-
 
 def on_device(mass_per_volume, motion_speed, agitation_energy, shear_deviatoric, thermal_current_array):
     def moved(a):
@@ -496,15 +506,14 @@
     gathered = (FIELDS, 2, 4, ROWS, COLS)
     dma = pltpu.SemaphoreType.DMA
     f32, bf16 = jnp.float32, jnp.bfloat16
-    own, par = pl.pallas_call(
+    out = pl.pallas_call(
         kernel,
-        out_shape=(
-            jax.ShapeDtypeStruct((FIELDS, ROWS, COLS), f32),
-            jax.ShapeDtypeStruct((FIELDS, ROWS, COLS), bf16),
-        ),
+        out_shape=jax.ShapeDtypeStruct((FIELDS, ROWS, 2 * COLS), f32),
         in_specs=[pl.BlockSpec(memory_space=pltpu.HBM)] * 5,
-        out_specs=(pl.BlockSpec(memory_space=pltpu.VMEM),) * 2,
+        out_specs=pl.BlockSpec(memory_space=pltpu.VMEM),
         scratch_shapes=[
+            pltpu.VMEM((FIELDS, ROWS, COLS), bf16),
+            pltpu.VMEM(full, f32),
             pltpu.VMEM(full, f32),
             pltpu.VMEM(full, f32),
             pltpu.VMEM(gathered, bf16),
@@ -544,20 +553,22 @@
             dma((FIELDS,)),
         ],
         compiler_params=pltpu.CompilerParams(
-            collective_id=0, has_side_effects=True, vmem_limit_bytes=66_500_000
+            collective_id=0, has_side_effects=True, vmem_limit_bytes=52_000_000
         ),
         name="sections",
     )(
-        mass_per_volume,
-        moved(motion_speed),
-        agitation_energy,
-        moved(shear_deviatoric),
-        moved(thermal_current_array),
+        *(
+            pltpu.with_memory_space_constraint(a, pltpu.HBM)
+            for a in (
+                mass_per_volume,
+                moved(motion_speed),
+                agitation_energy,
+                moved(shear_deviatoric),
+                moved(thermal_current_array),
+            )
+        )
     )
-    par = par.astype(f32)
-    lower = (lax.axis_index("gy") // 2) % 2 == 0
-    halves = [jnp.where(lower, own, par), jnp.where(lower, par, own)]
-    return jnp.transpose(jnp.concatenate(halves, axis=2), (1, 0, 2))
+    return jnp.transpose(out, (1, 0, 2))
 
 
 def solution(mesh):

time: 85.4 us -> 81.1 us (0.950); the launches traced: 84.1 us -> 81 us
  other arithmetic: 2.12 us -> 0 us
  Pallas kernels: 82 us -> 80.1 us
  local copies, waits for them, and re-layouts: 0 us -> 0.9 us
    pallas_call x1, Pallas kernels: 82 us -> 80.1 us  [on_device(): pl.pallas_call(kernel, out_shape=jax.ShapeDtypeStruct((FIELDS, ROWS, 2 *...]
    select_n x1 -> x0, other arithmetic: 1.15 us -> none  [on_device(): halves = [jnp.where(lower, own, par), jnp.where(lower, par, own)]]
    transpose x1 -> x0, other arithmetic: 0.97 us -> none  [on_device(): return jnp.transpose(jnp.concatenate(halves, axis=2), (1, 0, 2))]
    unnamed x0 -> x1, local copies, waits for them, and re-layouts: none -> 0.9 us
where the time goes in v3:
time: 81.1 us; the launch traced here: 81 us
  Pallas kernels  80.1 us (99%)
  local copies, waits for them, and re-layouts  0.9 us (1%)
    pallas_call x1, Pallas kernels, on_device(): pl.pallas_call(kernel, out_shape=jax.ShapeDtypeStruct((FIELDS, ROWS, 2 *...  80.1 us

profile of v3, /device:TPU:1, one launch (start us, length us, event | category | flops | bytes accessed | tf_op | source)
XLA Modules:
  0.0 81.0 jit_solution(3846186411756263261)
XLA Ops:
  0.0 80.1 %sections.1 = f32[13,64,256]{2,1,0:T(8,128)S(1)} custom-call(f32[64,256]{1,0:T(8,128)} %rho_ref.1, f32[3,64,256]{2,1,0:T(8,128)} %bitcast.6, f32[64,256]{1,0:T(8,128)} %temp_ref.1, f32[5,64,256]{2,1,0:T(8,128)} %bitcast.5, f32[3,64,256]{2,1,0:T(8,128)} %bitcast.7), custom_call_target="tpu_custom_call" | custom-call | tf_op jit(solution)/shard_map/sections/pallas_call | solution.py:509
  80.1 0.9 %copy.7 = f32[64,13,256]{2,0,1:T(8,128)} copy(f32[64,13,256]{2,0,1:T(8,128)S(1)} %bitcast.4) | data formatting | bytes 1703936

commit v4 on v3

--- a/solution.py
+++ b/solution.py
@@ -23,7 +23,7 @@
 COLS = 128
 TILE = 16
 PARTS = ROWS // TILE
-LEAD = 3
+LEAD = 2
 
 SPREAD = [(160.0, 1.25)] + [(40.0, 0.0)] * 3 + [(160.0, 1.25)] + [(50.0, 0.0)] * 8
 
@@ -87,29 +87,25 @@
 def edges(f, lane):
     out = jnp.zeros_like(f[0])
     for m in range(FIELDS):
-        a = pltpu.roll(f[m], 3 * m, 1) if m else f[m]
-        out = jnp.where((lane >= 3 * m) & (lane < 3 * m + 3), a, out)
-        b = pltpu.roll(f[m], 43 + 3 * m, 1)
-        out = jnp.where((lane >= 40 + 3 * m) & (lane < 43 + 3 * m), b, out)
+        moved = pltpu.roll(f[m], 6 * m + 3, 1)
+        out = jnp.where((lane >= 6 * m) & (lane < 6 * m + 6), moved, out)
     return out
 
 
 def mend(diff, lane):
-    low = lane < 40
-    place = jnp.where(low, lane, lane - 40) % 3
+    place = lane % 6
     a1, a2, a3 = coeffs
-    right = a3 * diff
-    right += jnp.where(place >= 1, a2, 0.0) * pltpu.roll(diff, 1, 1)
-    right += jnp.where(place >= 2, a1, 0.0) * pltpu.roll(diff, 2, 1)
-    left = a3 * diff
-    left += jnp.where(place <= 1, a2, 0.0) * pltpu.roll(diff, COLS - 1, 1)
-    left += jnp.where(place == 0, a1, 0.0) * pltpu.roll(diff, COLS - 2, 1)
-    return jnp.where(low, right, -left)
+    right = a3 * pltpu.roll(diff, COLS - 3, 1)
+    right += jnp.where(place >= 1, a2, 0.0) * pltpu.roll(diff, COLS - 2, 1)
+    right += jnp.where(place >= 2, a1, 0.0) * pltpu.roll(diff, COLS - 1, 1)
+    left = a3 * pltpu.roll(diff, 3, 1)
+    left += jnp.where(place <= 4, a2, 0.0) * pltpu.roll(diff, 2, 1)
+    left += jnp.where(place <= 3, a1, 0.0) * pltpu.roll(diff, 1, 1)
+    return jnp.where(place < 3, right, -left)
 
 
 def spread(packed, m, lane):
-    a = jnp.where(lane >= 125, pltpu.roll(packed, 125 - 3 * m, 1), 0.0)
-    return a + jnp.where(lane < 3, pltpu.roll(packed, 88 - 3 * m, 1), 0.0)
+    return jnp.where((lane >= 125) | (lane < 3), pltpu.roll(packed, 125 - 6 * m, 1), 0.0)
 
 
 def sine(x):
@@ -341,13 +337,13 @@
             gather_part(t, k).start()
         first(pl.multiple_of(pbase + r, TILE), u)
 
-    low, high = pl.ds(0, 40), pl.ds(40, 40)
+    packed = pl.ds(0, 80)
 
     def send_edges(GT, H, ssem, rsem):
-        GT[...] = G[...].T
+        GT[...] = G[...].T.astype(jnp.bfloat16)
         copies = [
-            remote(GT.at[low], H.at[0], ssem.at[0], rsem.at[0], left_to),
-            remote(GT.at[high], H.at[1], ssem.at[1], rsem.at[1], right_to),
+            remote(GT.at[packed], H.at[0], ssem.at[0], rsem.at[0], left_to),
+            remote(GT.at[packed], H.at[1], ssem.at[1], rsem.at[1], right_to),
         ]
         for copy in copies:
             copy.start()
@@ -374,8 +370,8 @@
     def receive_edges(copies, H):
         for copy in copies:
             copy.wait_recv()
-        TT[low, :] = H[0]
-        TT[high, :] = H[1]
+        place = lax.broadcasted_iota(jnp.int32, (80, 128), 0) % 6
+        TT[packed, :] = jnp.where(place >= 3, H[0].astype(jnp.float32), H[1].astype(jnp.float32))
         TT[pl.ds(80, 48), :] = jnp.zeros((48, COLS), jnp.float32)
         TT[...] = TT[...].T
 
@@ -527,10 +523,10 @@
             pltpu.VMEM(full, f32),
             pltpu.VMEM((256, 512), bf16),
             pltpu.VMEM((128, COLS), f32),
-            pltpu.VMEM((COLS, 128), f32),
-            pltpu.VMEM((COLS, 128), f32),
-            pltpu.VMEM((2, 40, 128), f32),
-            pltpu.VMEM((2, 40, 128), f32),
+            pltpu.VMEM((COLS, 128), bf16),
+            pltpu.VMEM((COLS, 128), bf16),
+            pltpu.VMEM((2, 80, 128), bf16),
+            pltpu.VMEM((2, 80, 128), bf16),
             pltpu.VMEM((128, 128), f32),
             pltpu.VMEM((2, FIELDS, ROWS, COLS), f32),
             pltpu.VMEM((FIELDS, ROWS, COLS), bf16),

time: 81.1 us -> 80.7 us (level)
  no operation moved by 1% of the time
where the time goes in v4:
time: 80.7 us; the launch traced here: 80.6 us
  Pallas kernels  79.7 us (99%)
  local copies, waits for them, and re-layouts  0.9 us (1%)
    pallas_call x1, Pallas kernels, on_device(): pl.pallas_call(kernel, out_shape=jax.ShapeDtypeStruct((FIELDS, ROWS, 2 *...  79.7 us

profile of v4, /device:TPU:1, one launch (start us, length us, event | category | flops | bytes accessed | tf_op | source)
XLA Modules:
  0.0 80.6 jit_solution(18230086513124859160)
XLA Ops:
  0.0 79.7 %sections.1 = f32[13,64,256]{2,1,0:T(8,128)S(1)} custom-call(f32[64,256]{1,0:T(8,128)} %rho_ref.1, f32[3,64,256]{2,1,0:T(8,128)} %bitcast.6, f32[64,256]{1,0:T(8,128)} %temp_ref.1, f32[5,64,256]{2,1,0:T(8,128)} %bitcast.5, f32[3,64,256]{2,1,0:T(8,128)} %bitcast.7), custom_call_target="tpu_custom_call" | custom-call | tf_op jit(solution)/shard_map/sections/pallas_call | solution.py:505
  79.7 0.9 %copy.7 = f32[64,13,256]{2,0,1:T(8,128)} copy(f32[64,13,256]{2,0,1:T(8,128)S(1)} %bitcast.4) | data formatting | bytes 1703936

commit v5 on v4

--- a/solution.py
+++ b/solution.py
@@ -403,9 +403,14 @@
         block = F2.at[m, :, x]
         return remote(block, block, f2_s.at[m, k], f2_r.at[m, k], peers[k])
 
+    @pl.loop(0, LEAD)
+    def _(m):
+        for k in range(3):
+            gather2(m, k).start()
+
     halos2 = send_edges(GT2, H2, g_s, g_r)
 
-    @pl.loop(0, FIELDS)
+    @pl.loop(LEAD, FIELDS)
     def _(m):
         for k in range(3):
             gather2(m, k).start()

time: 80.7 us -> 80.4 us (level)
  no operation moved by 1% of the time
where the time goes in v5:
time: 80.4 us; the launch traced here: 80.2 us
  Pallas kernels  79.3 us (99%)
  local copies, waits for them, and re-layouts  0.9 us (1%)
    pallas_call x1, Pallas kernels, on_device(): pl.pallas_call(kernel, out_shape=jax.ShapeDtypeStruct((FIELDS, ROWS, 2 *...  79.3 us

profile of v5, /device:TPU:1, one launch (start us, length us, event | category | flops | bytes accessed | tf_op | source)
XLA Modules:
  0.0 80.2 jit_solution(11491634368182138869)
XLA Ops:
  0.0 79.3 %sections.1 = f32[13,64,256]{2,1,0:T(8,128)S(1)} custom-call(f32[64,256]{1,0:T(8,128)} %rho_ref.1, f32[3,64,256]{2,1,0:T(8,128)} %bitcast.6, f32[64,256]{1,0:T(8,128)} %temp_ref.1, f32[5,64,256]{2,1,0:T(8,128)} %bitcast.5, f32[3,64,256]{2,1,0:T(8,128)} %bitcast.7), custom_call_target="tpu_custom_call" | custom-call | tf_op jit(solution)/shard_map/sections/pallas_call | solution.py:510
  79.3 0.9 %copy.7 = f32[64,13,256]{2,0,1:T(8,128)} copy(f32[64,13,256]{2,0,1:T(8,128)S(1)} %bitcast.4) | data formatting | bytes 1703936
